TPU v7x, 512 devices: a whole 4x8x8 slice. The times are simulated.
512 devices in a mesh: dp: 32 (over x, y), table: 16 (over z, core).
Axes of the slice: x: 4, y: 8, z: 8, core: 2. Of those that a mesh axis runs over, the one named last changes fastest.
Arguments:
- table: bfloat16 [12288, 512], P('table'), may hold values from -6 to 6
- history_shard: int32 [512, 256, 1], P(('dp', 'table')), may hold values from 0 to 15; in each aligned block of 256 rows (0 to 255, 256 to 511, ..., all dimensions but the last counted through in order) at most 32 rows name the same one
- history_row: int32 [512, 256], P(('dp', 'table')), may hold values from 0 to 767
- lengths: int32 [512], P(('dp', 'table')), may hold values from 1 to 256, 98304 in all
- w_in: bfloat16 [512, 2048], replicated, may hold values from -0.25 to 0.25
- w_out: bfloat16 [512, 512], replicated, may hold values from -0.25 to 0.25
- cotangent: bfloat16 [512, 256, 512], P(('dp', 'table')), may hold values from -6 to 6
Outputs:
- table_grad: float32 [12288, 512], P('table')
- dense_grad: bfloat16 [512, 512], replicated
Inputs may be any that keep to these rules, and one draw needn't show every extreme that they name: `history_shard`: among the 256 history slots of one device's samples, at most 32 name one table shard, and that bound is met by some shard in some device's slots. `lengths`: some sample has the full length 256.
All inputs are finite; a program needn't handle non-finite values. No bound on the sum of `lengths` on one device may be relied on, other than what follows from the above.
Results may differ from a plain program's by a relative error of at most 0.017.
Values may be sent and summed in bfloat16 or wider, within the bound.
A program may use at most 64 MiB of HBM per device.

v0:
```python
import math
import jax
import jax.numpy as jnp
from jax import lax
from jax.sharding import PartitionSpec as P

HEADS = 4


def layer_norm(values):
    average = jnp.mean(values, axis=-1, keepdims=True)
    centred = values - average
    variance = jnp.mean(centred * centred, axis=-1, keepdims=True)
    return centred * lax.rsqrt(variance + 1e-06)


def hstu_layer(embedded, w_in, w_out, lengths):
    samples_here, seq_span, model_width = embedded.shape
    head_dim = model_width // HEADS
    normed = layer_norm(embedded.astype(jnp.float32)).astype(jnp.bfloat16)
    projected = jax.nn.silu(
        jnp.dot(
            normed.reshape(samples_here * seq_span, model_width),
            w_in,
            preferred_element_type=jnp.float32,
        )
    )
    gate_part = projected[:, :model_width]
    shaped = (samples_here, seq_span, HEADS, head_dim)
    values = projected[:, model_width : 2 * model_width].astype(jnp.bfloat16).reshape(shaped)
    queries = projected[:, 2 * model_width : 3 * model_width].astype(jnp.bfloat16).reshape(shaped)
    keys = projected[:, 3 * model_width :].astype(jnp.bfloat16).reshape(shaped)
    scores = jnp.einsum(
        "blhd,bmhd->bhlm", queries.astype(jnp.float32), keys.astype(jnp.float32)
    ) * head_dim ** (-0.5)
    positions = jnp.arange(seq_span)
    live_keys = (positions[None, None, :] <= positions[None, :, None]) & (
        positions[None, None, :] < lengths[:, None, None]
    )
    weights = (
        jnp.where(live_keys[:, None], jax.nn.silu(scores), 0.0)
        / lengths.astype(jnp.float32)[:, None, None, None]
    )
    weights = weights.astype(jnp.bfloat16)
    attended = jnp.einsum(
        "bhlm,bmhd->blhd", weights.astype(jnp.float32), values.astype(jnp.float32)
    ).reshape(samples_here * seq_span, model_width)
    mixed = (layer_norm(attended) * gate_part).astype(jnp.bfloat16)
    output = jnp.dot(mixed, w_out, preferred_element_type=jnp.float32) + embedded.reshape(
        -1, model_width
    ).astype(jnp.float32)
    return (output, mixed)


def per_device(table, history_shard, history_row, lengths, w_in, w_out, cotangent):
    shard_rows, model_width = table.shape
    samples_here, seq_span = history_row.shape
    groups = lax.axis_size("table")
    slot_count = samples_here * seq_span
    capacity = 2 * slot_count // groups
    owners = history_shard[:, :, 0].reshape(-1)
    local_rows = history_row.reshape(-1)
    owner_hits = (owners[:, None] == jnp.arange(groups)[None, :]).astype(jnp.int32)
    slot_rank = jnp.sum((jnp.cumsum(owner_hits, axis=0) - owner_hits) * owner_hits, axis=1)
    position = owners * capacity + slot_rank
    requested = (
        jnp.zeros((groups * capacity,), jnp.int32)
        .at[position]
        .set(local_rows)
        .reshape(groups, capacity)
    )
    incoming = lax.all_to_all(requested, "table", split_axis=0, concat_axis=0, tiled=True).reshape(
        -1
    )
    global_rows = owners * shard_rows + local_rows
    piece = lax.all_gather(table, "table", axis=0, tiled=True)
    inside = (global_rows >= 0) & (global_rows < piece.shape[0])
    taken = piece[jnp.clip(global_rows, 0, piece.shape[0] - 1)].astype(jnp.float32)
    embedded = jnp.where(inside[:, None], taken, 0.0).astype(jnp.bfloat16)
    embedded = embedded.reshape(samples_here, seq_span, model_width)
    output, pullback, mixed = jax.vjp(
        lambda rows_in: hstu_layer(rows_in, w_in, w_out, lengths), embedded, has_aux=True
    )
    row_live = jnp.arange(seq_span)[None, :] < lengths[:, None]
    grad_seed = jnp.where(row_live[:, :, None], cotangent, jnp.zeros_like(cotangent))
    flat_seed = grad_seed.reshape(-1, model_width)
    (row_grad,) = pullback(flat_seed.astype(jnp.float32))
    dense_part = jnp.dot(mixed.T, flat_seed, preferred_element_type=jnp.float32)
    outgoing = (
        jnp.zeros((groups * capacity, model_width), jnp.bfloat16)
        .at[position]
        .set(row_grad.reshape(-1, model_width))
    )
    arrived = lax.all_to_all(
        outgoing.reshape(groups, capacity, model_width),
        "table",
        split_axis=0,
        concat_axis=0,
        tiled=True,
    )
    local_grad = (
        jnp.zeros((shard_rows, model_width), jnp.float32)
        .at[incoming]
        .add(arrived.reshape(-1, model_width).astype(jnp.float32))
    )
    total_slots = slot_count * lax.axis_size("dp") * groups
    grad_scale = 1.0 / math.sqrt(total_slots)
    table_grad = lax.psum(local_grad, "dp")
    dense_total = lax.psum(dense_part, ("dp", "table"))
    dense_grad = (dense_total * grad_scale).astype(jnp.bfloat16)
    return (table_grad, dense_grad)


def solution(mesh):
    in_specs = (
        P("table", None),
        P(("dp", "table"), None, None),
        P(("dp", "table"), None),
        P(("dp", "table")),
        P(),
        P(),
        P(("dp", "table"), None, None),
    )
    out_specs = (P("table", None), P())
    return jax.shard_map(
        per_device, mesh=mesh, in_specs=in_specs, out_specs=out_specs, check_vma=False
    )
```

profile of v0, /device:TPU:64, one launch (start us, length us, event | category | flops | bytes accessed | tf_op | source)
XLA Modules:
  0.0 582.9 jit_solution(10138484838293075610)
XLA Ops:
  7.2 0.7 all-gather.2.cloned.1.call-update
  7.9 0.7 fusion.64
  9.4 0.8 fusion.63
  10.2 0.7 compare_select_fusion.1
  10.9 1.6 scatter_custom_fusion
  12.4 0.7 all_to_all.9
  13.1 10.0 %all-to-all-start = ((s32[16,1,32]{2,1,0:T(1,128)}), s32[16,1,32]{2,1,0:T(1,128)S(1)}, u32[]{:S(2)}, u32[]{:S(2)}) async-start(s32[16,1,32]{2,1,0:T(1,128)} %all_to_all.9), calls=%async_computation | async-start | bytes 16384 | tf_op jit(solution)/shard_map/all_to_all | solution.py:72
  23.8 0.7 compare_and_fusion
  24.5 66.3 %all-gather.2.cloned.1.call-done = bf16[12288,512]{1,0:T(8,128)(2,1)} async-done(((bf16[768,512]{1,0:T(8,128)(2,1)}), bf16[12288,512]{1,0:T(8,128)(2,1)}) %all-gather.2.cloned.1.call-update) | async-done | bytes 12582928 | tf_op jit(solution)/shard_map/all_gather | solution.py:76
  90.8 7.4 %gather_fusion = bf16[256,512]{1,0:T(8,128)(2,1)S(1)} fusion(bf16[12288,512]{1,0:T(8,128)(2,1)} %all-gather.2.cloned.1.call-done, s32[1024]{0:T(1024)S(1)} %pad_clamp_fusion), kind=kCustom, calls=%fused_computation | custom fusion | bytes 525312 | tf_op jit(solution)/shard_map/gather | solution.py:78
  98.7 2.8 fusion.76
  101.5 0.8 slice_bitcast_fusion
  102.5 1.6 divide_convert_fusion
  105.1 1.7 multiply_reduce_fusion.1
  106.9 2.1 fusion.75
  109.2 2.0 fusion.26
  111.5 1.0 fusion.79
  112.5 0.9 fusion.81
  113.6 1.8 copy.38
  115.4 1.8 copy.39
  117.2 3.4 multiply_reduce_fusion
  120.6 1.0 fusion.74
  121.6 2.9 scatter_custom_fusion.1
  124.5 6.9 %all-to-all-start.1 = ((bf16[16,32,512]{2,1,0:T(8,128)(2,1)}), bf16[16,32,512]{2,1,0:T(8,128)(2,1)}, u32[]{:S(2)}, u32[]{:S(2)}) async-start(bf16[16,32,512]{2,1,0:T(8,128)(2,1)} %bitcast.120), calls=%async_computation.1 | async-start | bytes 1048576 | tf_op jit(solution)/shard_map/all_to_all | solution.py:94
  131.6 2.5 fusion.45
  134.7 0.7 reduce.15
  135.4 10.4 %all-to-all-done.1 = bf16[16,32,512]{2,1,0:T(8,128)(2,1)} async-done(((bf16[16,32,512]{2,1,0:T(8,128)(2,1)}), bf16[16,32,512]{2,1,0:T(8,128)(2,1)}, u32[]{:S(2)}, u32[]{:S(2)}) %all-to-all-start.1) | async-done | bytes 524320 | tf_op jit(solution)/shard_map/all_to_all | solution.py:94
  145.8 5.5 scatter_custom_fusion.2
  151.3 258.6 %all-reduce.9.cloned.1.call-done = f32[512,512]{1,0:T(8,128)} async-done(((f32[512,512]{1,0:T(8,128)}), f32[512,512]{1,0:T(8,128)}) %all-reduce.9.cloned.1.call-update) | async-done | bytes 1048592 | tf_op jit(solution)/shard_map/psum | solution.py:109
  409.9 2.1 multiply_convert_fusion
  412.0 161.6 %all-reduce.7.cloned.1.call-done = f32[768,512]{1,0:T(8,128)} async-done(((f32[768,512]{1,0:T(8,128)}), f32[768,512]{1,0:T(8,128)}) %all-reduce.7.cloned.1.call-update) | async-done | bytes 1572880 | tf_op jit(solution)/shard_map/psum | solution.py:108
  573.7 2.7 copy.58
  (52 shorter events, 4.1 us)
Async XLA Ops:
  7.2 91.5 %copy-start = (bf16[512,2048]{1,0:T(8,128)(2,1)S(1)}, bf16[512,2048]{1,0:T(8,128)(2,1)}, u32[]{:S(2)}) copy-start(bf16[512,2048]{1,0:T(8,128)(2,1)} %param.11) | copy-start | bytes 6291460
  7.2 83.6 %all-gather.2.cloned.1.call-start = ((), (), s32[]{:S(2)}) async-start(), calls=%async_computation.2 | async-start | bytes 13369344 | tf_op jit(solution)/shard_map/all_gather | solution.py:76
  13.1 111.4 %all-to-all-start = ((s32[16,1,32]{2,1,0:T(1,128)}), s32[16,1,32]{2,1,0:T(1,128)S(1)}, u32[]{:S(2)}, u32[]{:S(2)}) async-start(s32[16,1,32]{2,1,0:T(1,128)} %all_to_all.9), calls=%async_computation | async-start | bytes 16384 | tf_op jit(solution)/shard_map/all_to_all | solution.py:72
  102.4 1.8 copy-start.4
  102.5 1.6 copy-start.6
  102.5 1.6 copy-start.8
  104.1 0.8 copy-start.2
  109.2 2.1 copy-start.5
  109.2 2.3 copy-start.7
  111.2 1.3 copy-start.3
  117.2 4.4 copy-start.1
  124.5 21.3 %all-to-all-start.1 = ((bf16[16,32,512]{2,1,0:T(8,128)(2,1)}), bf16[16,32,512]{2,1,0:T(8,128)(2,1)}, u32[]{:S(2)}, u32[]{:S(2)}) async-start(bf16[16,32,512]{2,1,0:T(8,128)(2,1)} %bitcast.120), calls=%async_computation.1 | async-start | bytes 1048576 | tf_op jit(solution)/shard_map/all_to_all | solution.py:94
  131.4 278.5 %all-reduce.9.cloned.1.call-start = ((), (), s32[]{:S(2)}) async-start(), calls=%async_computation.4 | async-start | bytes 2097152 | tf_op jit(solution)/shard_map/psum | solution.py:109
  134.1 439.6 %all-reduce.7.cloned.1.call-start = ((), (), s32[]{:S(2)}) async-start(), calls=%async_computation.3 | async-start | bytes 3145728 | tf_op jit(solution)/shard_map/psum | solution.py:108
Sparse Core Ops, SparseCore 0:
  10.1 80.5 all-gather.1
  137.3 272.5 all-reduce.8
  414.3 159.3 all-reduce.6
where the time goes:
time: 584 us; the launch traced here: 583 us
  waiting for transfers between devices  498 us (85%)
  local copies, waits for them, and re-layouts  18.5 us (3%)
  other arithmetic  18.5 us (3%)
  starting transfers between devices  17.1 us (3%)
  matrix products  16.5 us (3%)
  between operations  14.6 us (2%)
    psum x1, waiting for transfers between devices, per_device(): dense_total = lax.psum(dense_part, ('dp', 'table'))  259 us
    psum x1, waiting for transfers between devices, per_device(): table_grad = lax.psum(local_grad, 'dp')  162 us
    all_gather x1, waiting for transfers between devices, per_device(): piece = lax.all_gather(table, 'table', axis=0, tiled=True)  66.3 us
  transfers between devices with their start and end apart: 5, of which 4 were waited for; matrix products, arithmetic and copies ran while one was open for 9% of the time, Pallas kernels for 0%

commit v1 on v0

--- a/solution.py
+++ b/solution.py
@@ -106,7 +106,8 @@
     total_slots = slot_count * lax.axis_size("dp") * groups
     grad_scale = 1.0 / math.sqrt(total_slots)
     table_grad = lax.psum(local_grad, "dp")
-    dense_total = lax.psum(dense_part, ("dp", "table"))
+    half = lax.psum(dense_part, "dp")
+    dense_total = lax.psum(half, "table")
     dense_grad = (dense_total * grad_scale).astype(jnp.bfloat16)
     return (table_grad, dense_grad)
 

time: 584 us -> 448 us (0.77)
  the two profiles are of different devices: /device:TPU:64 before, /device:TPU:1 now
where the time goes in v1:
time: 448 us; the launch traced here: 447 us
  waiting for transfers between devices  364 us (81%)
  other arithmetic  18.6 us (4%)
  local copies, waits for them, and re-layouts  17 us (4%)
  matrix products  16.5 us (4%)
  starting transfers between devices  16.4 us (4%)
  between operations  14.6 us (3%)
    psum x1, waiting for transfers between devices, per_device(): table_grad = lax.psum(local_grad, 'dp')  159 us
    psum x1, waiting for transfers between devices, per_device(): dense_total = lax.psum(half, 'table')  121 us
    all_gather x1, waiting for transfers between devices, per_device(): piece = lax.all_gather(table, 'table', axis=0, tiled=True)  68.8 us
    all_to_all x1, waiting for transfers between devices, per_device(): lax.all_to_all(outgoing.reshape(groups, capacity, model_width), 'table',...  13.4 us
    all_to_all x1, starting transfers between devices, per_device(): lax.all_to_all(requested, 'table', split_axis=0, concat_axis=0, tiled=True)  11.8 us
  transfers between devices with their start and end apart: 5, of which 4 were waited for; matrix products, arithmetic and copies ran while one was open for 9% of the time, Pallas kernels for 0%

profile of v1, /device:TPU:1, one launch (start us, length us, event | category | flops | bytes accessed | tf_op | source)
XLA Modules:
  0.0 446.8 jit_solution(6523637485365780998)
XLA Ops:
  7.2 0.7 all-gather.2.cloned.1.call-update
  7.9 0.7 fusion.64
  9.4 0.8 fusion.63
  10.2 0.7 compare_select_fusion.1
  10.9 1.6 scatter_custom_fusion
  12.4 0.7 all_to_all.9
  13.1 11.8 %all-to-all-start = ((s32[16,1,32]{2,1,0:T(1,128)}), s32[16,1,32]{2,1,0:T(1,128)S(1)}, u32[]{:S(2)}, u32[]{:S(2)}) async-start(s32[16,1,32]{2,1,0:T(1,128)} %all_to_all.9), calls=%async_computation | async-start | bytes 16384 | tf_op jit(solution)/shard_map/all_to_all | solution.py:72
  25.6 0.7 compare_and_fusion
  26.4 68.8 %all-gather.2.cloned.1.call-done = bf16[12288,512]{1,0:T(8,128)(2,1)} async-done(((bf16[768,512]{1,0:T(8,128)(2,1)}), bf16[12288,512]{1,0:T(8,128)(2,1)}) %all-gather.2.cloned.1.call-update) | async-done | bytes 12582928 | tf_op jit(solution)/shard_map/all_gather | solution.py:76
  95.2 7.4 %gather_fusion = bf16[256,512]{1,0:T(8,128)(2,1)S(1)} fusion(bf16[12288,512]{1,0:T(8,128)(2,1)} %all-gather.2.cloned.1.call-done, s32[1024]{0:T(1024)S(1)} %pad_clamp_fusion), kind=kCustom, calls=%fused_computation | custom fusion | bytes 525312 | tf_op jit(solution)/shard_map/gather | solution.py:78
  103.1 2.8 fusion.76
  105.9 0.8 slice_bitcast_fusion
  107.0 1.6 divide_convert_fusion
  109.5 1.7 multiply_reduce_fusion.1
  111.3 2.1 fusion.75
  113.6 2.0 fusion.26
  115.9 1.0 fusion.79
  116.9 0.9 fusion.81
  118.0 1.8 copy.38
  119.8 1.8 copy.39
  121.6 3.4 multiply_reduce_fusion
  125.0 1.0 fusion.74
  126.0 2.9 scatter_custom_fusion.1
  128.9 4.3 all-to-all-start.1
  134.0 0.7 reduce.15
  134.7 2.5 fusion.45
  137.2 13.4 %all-to-all-done.1 = bf16[16,32,512]{2,1,0:T(8,128)(2,1)} async-done(((bf16[16,32,512]{2,1,0:T(8,128)(2,1)}), bf16[16,32,512]{2,1,0:T(8,128)(2,1)}, u32[]{:S(2)}, u32[]{:S(2)}) %all-to-all-start.1) | async-done | bytes 524320 | tf_op jit(solution)/shard_map/all_to_all | solution.py:94
  150.6 5.4 %scatter_custom_fusion.2 = f32[768,512]{1,0:T(8,128)} fusion(s32[512]{0:T(512)S(1)} %bitcast.137, bf16[512,512]{1,0:T(8,128)(2,1)} %bitcast.42, f32[]{:T(128)} %constant.15.clone.1), kind=kCustom, calls=%fused_computation.35 | custom fusion | flops 524288 | bytes 2097156 | tf_op jit(solution)/shard_map/scatter-add | solution.py:104
  156.2 159.3 %all-reduce.10.cloned.1.call-done = (f32[768,512]{1,0:T(8,128)}, f32[512,512]{1,0:T(8,128)}) async-done(((f32[768,512]{1,0:T(8,128)}, f32[512,512]{1,0:T(8,128)}), (f32[768,512]{1,0:T(8,128)}, f32[512,512]{1,0:T(8,128)})) %all-reduce.10.cloned.1.call-update) | async-done | bytes 2621456 | tf_op jit(solution)/shard_map/psum | solution.py:108
  315.5 121.4 %all-reduce.8.cloned.1.call-done = f32[512,512]{1,0:T(8,128)} async-done(((f32[512,512]{1,0:T(8,128)}), f32[512,512]{1,0:T(8,128)}) %all-reduce.8.cloned.1.call-update) | async-done | bytes 1048592 | tf_op jit(solution)/shard_map/psum | solution.py:110
  436.9 2.3 multiply_convert_fusion
  439.1 1.1 copy.59
  (54 shorter events, 4.1 us)
Async XLA Ops:
  7.2 95.9 %copy-start = (bf16[512,2048]{1,0:T(8,128)(2,1)S(1)}, bf16[512,2048]{1,0:T(8,128)(2,1)}, u32[]{:S(2)}) copy-start(bf16[512,2048]{1,0:T(8,128)(2,1)} %param.11) | copy-start | bytes 6291460
  7.2 88.0 %all-gather.2.cloned.1.call-start = ((), (), s32[]{:S(2)}) async-start(), calls=%async_computation.2 | async-start | bytes 13369344 | tf_op jit(solution)/shard_map/all_gather | solution.py:76
  13.1 115.8 %all-to-all-start = ((s32[16,1,32]{2,1,0:T(1,128)}), s32[16,1,32]{2,1,0:T(1,128)S(1)}, u32[]{:S(2)}, u32[]{:S(2)}) async-start(s32[16,1,32]{2,1,0:T(1,128)} %all_to_all.9), calls=%async_computation | async-start | bytes 16384 | tf_op jit(solution)/shard_map/all_to_all | solution.py:72
  106.8 1.8 copy-start.5
  106.9 1.6 copy-start.7
  106.9 1.6 copy-start.9
  108.5 0.8 copy-start.2
  113.6 2.1 copy-start.6
  113.6 2.3 copy-start.8
  115.6 1.3 copy-start.3
  121.6 4.4 copy-start.1
  128.9 21.7 %all-to-all-start.1 = ((bf16[16,32,512]{2,1,0:T(8,128)(2,1)}), bf16[16,32,512]{2,1,0:T(8,128)(2,1)}, u32[]{:S(2)}, u32[]{:S(2)}) async-start(bf16[16,32,512]{2,1,0:T(8,128)(2,1)} %bitcast.120), calls=%async_computation.1 | async-start | bytes 1048576 | tf_op jit(solution)/shard_map/all_to_all | solution.py:94
  133.2 182.3 %all-reduce.10.cloned.1.call-start = ((), (), s32[]{:S(2)}) async-start(), calls=%async_computation.4 | async-start | bytes 5242880 | tf_op jit(solution)/shard_map/psum | solution.py:108
  156.1 280.8 %all-reduce.8.cloned.1.call-start = ((), (), s32[]{:S(2)}) async-start(), calls=%async_computation.3 | async-start | bytes 2097152 | tf_op jit(solution)/shard_map/psum | solution.py:110
  436.9 2.3 copy-start.4
Sparse Core Ops, SparseCore 0:
  10.1 84.9 all-gather.1
  156.2 159.2 all-reduce.9
  317.8 119.0 all-reduce.7
